TPU v7x, 32 devices: a whole 2x2x4 slice. The times are simulated.
32 devices in a mesh: group: 4 (over z), dev: 8 (over y, x, core).
Axes of the slice: x: 2, y: 2, z: 4, core: 2. Of those that a mesh axis runs over, the one named last changes fastest.
Arguments:
- positions: float32 [3, 1024, 256], P(None, ('group', 'dev')), may hold values from -3 to 3
- velocities: float32 [3, 1024, 256], P(None, ('group', 'dev')), may hold values from -3 to 3
- masses: float32 [1024, 256], P(('group', 'dev')), may hold values from 0.005 to 0.05
- counts: int32 [1024], P(('group', 'dev')), may hold values from 64 to 256, as said below
- walls: int32 [1024, 256], P(('group', 'dev')), may hold values 0 or 1
- neighbours: int32 [1024, 3], P(('group', 'dev')), may hold values from 0 to 55, as said below
- send_cells: int32 [4, 8, 8, 2], P('group', 'dev'), may hold values from -1 to 31, as said below
- owners: int32 [4, 256], P('group'), may hold values from 0 to 7, as said below
Outputs:
- new_state: float32 [6, 1024, 256], P(None, ('group', 'dev'))
- new_density: float32 [1024, 256], P(('group', 'dev'))
Inputs may be any that keep to these rules, and one draw needn't show every extreme that they name: `counts`: every device holds at least one cell with 256 particles. `send_cells`: A device never sends to itself; slot 0 to every other device of its group holds a cell. `neighbours`: A cell never names its own row; on each device every rim row and every filled incoming slot is named at least once, and no empty incoming slot is named. `owners`: each device of a group owns exactly 32 cells afterwards; each device keeps 32 - 2 * 2 of its cells and hands exactly 2 cells to each of 2 other devices of its group, and none to the rest.
All inputs are finite; a program needn't handle non-finite values. No bound on the sum of `walls` on one device may be relied on, other than what follows from the above.
Results may differ from a plain program's by a relative error of at most 0.0003.
Values sent between devices are 32-bit elements; how exact they have to be, the bound alone decides.
A program may use at most 64 MiB of HBM per device.

v0:
```python
import jax
import jax.numpy as jnp
from jax import lax
from jax.sharding import PartitionSpec as P

RIM_CELLS = 4
SUPPORT = 4.0
STIFFNESS = 2.0
REST_DENSITY = 0.8
VISCOSITY = 0.5
COHESION = 0.3
ADHESION = 0.8
GRAVITY = 1.0
TIME_STEP = 0.5


def with_halo(cells, sides, width):
    for axis, dim in sides:
        count = lax.axis_size(axis)
        ends = count - 1
        head = lax.slice_in_dim(cells, 0, width, axis=dim)
        tail = lax.slice_in_dim(cells, cells.shape[dim] - width, cells.shape[dim], axis=dim)
        cells = jnp.concatenate(
            [
                lax.ppermute(tail, axis, [(i, (i + 1) % count) for i in range(ends)]),
                cells,
                lax.ppermute(head, axis, [((i + 1) % count, i) for i in range(ends)]),
            ],
            axis=dim,
        )
    return cells


def pair_density(own_pos, lookup, columns):
    remote = lookup[:, columns, :]
    distance = jnp.zeros(
        (own_pos.shape[1], own_pos.shape[2], columns.shape[1], lookup.shape[2]), jnp.float32
    )
    for component in range(3):
        offset = own_pos[component][:, :, None, None] - remote[component][:, None, :, :]
        distance = distance + offset * offset
    weight = jnp.maximum(1.0 - distance / SUPPORT, 0.0)
    return jnp.sum(remote[3][:, None, :, :] * weight * weight * weight, axis=(2, 3))


def pair_force(own_pos, own_vel, own_q, lookup, columns):
    remote = lookup[:, columns, :]
    distance = jnp.zeros(
        (own_pos.shape[1], own_pos.shape[2], columns.shape[1], lookup.shape[2]), jnp.float32
    )
    offsets = []
    for component in range(3):
        offset = own_pos[component][:, :, None, None] - remote[component][:, None, :, :]
        offsets.append(offset)
        distance = distance + offset * offset
    weight = jnp.maximum(1.0 - distance / SUPPORT, 0.0)
    cube = weight * weight * weight
    pushes = (
        remote[6][:, None]
        * (own_q[:, :, None, None] + remote[8][:, None])
        * (6.0 / SUPPORT)
        * weight
        * weight
        - remote[7][:, None] * weight
    )
    damping = VISCOSITY * remote[6][:, None] * cube
    total_damping = jnp.sum(damping, axis=(2, 3))
    rows = []
    for component in range(3):
        rows.append(
            jnp.sum(
                offsets[component] * pushes + damping * remote[3 + component][:, None], axis=(2, 3)
            )
            - own_vel[component] * total_damping
        )
    return jnp.stack(rows, 0)


def shards(positions, velocities, masses, counts, walls, neighbours, send_cells, owners):
    cell_count = positions.shape[1]
    block_width = positions.shape[2]
    peer_count = lax.axis_size("dev")
    particle_slot = lax.broadcasted_iota(jnp.int32, (cell_count, block_width), 1)
    active = (particle_slot < counts[:, None]).astype(jnp.float32)
    wall_mask = walls.astype(jnp.float32) * active
    fluid_mask = active - wall_mask
    mass_eff = masses * active
    bond = mass_eff * (COHESION + (ADHESION - COHESION) * wall_mask)
    send_list = send_cells[0, 0].reshape(-1)
    present = (send_list >= 0).astype(jnp.float32)
    chosen = jnp.maximum(send_list, 0)

    def outgoing(field):
        return field[:, chosen, :] * present[None, :, None]

    def joined(padded, arrived):
        return jnp.concatenate([padded, arrived], 1)

    dens_field = jnp.concatenate([positions, mass_eff[None]], 0)
    dens_table = joined(
        with_halo(dens_field, (("group", 1),), RIM_CELLS),
        lax.all_to_all(outgoing(dens_field), "dev", split_axis=1, concat_axis=1, tiled=True),
    )
    cell_blocks = jnp.arange(cell_count, dtype=jnp.int32).reshape(-1, 4)

    def density_block(cell_ids):
        columns = jnp.concatenate([RIM_CELLS + cell_ids[:, None], neighbours[cell_ids]], 1)
        return pair_density(positions[:, cell_ids, :], dens_table, columns)

    density = lax.map(density_block, cell_blocks).reshape(cell_count, block_width)
    safe_rho = active * density + (1.0 - active)
    pressure_q = active * STIFFNESS * (density - REST_DENSITY) / (safe_rho * safe_rho)
    force_field = jnp.concatenate(
        [positions, velocities, mass_eff[None], bond[None], pressure_q[None]], 0
    )
    force_table = joined(
        with_halo(force_field, (("group", 1),), RIM_CELLS),
        lax.all_to_all(outgoing(force_field), "dev", split_axis=1, concat_axis=1, tiled=True),
    )

    def force_block(cell_ids):
        columns = jnp.concatenate([RIM_CELLS + cell_ids[:, None], neighbours[cell_ids]], 1)
        return pair_force(
            positions[:, cell_ids, :],
            velocities[:, cell_ids, :],
            pressure_q[cell_ids],
            force_table,
            columns,
        )

    acceleration = lax.map(force_block, cell_blocks)
    acceleration = jnp.transpose(acceleration, (1, 0, 2, 3)).reshape(3, cell_count, block_width)
    gravity_vec = jnp.array([0.0, 0.0, GRAVITY], jnp.float32)[:, None, None]
    acceleration = acceleration - gravity_vec
    new_vel = velocities + TIME_STEP * fluid_mask[None] * acceleration
    new_pos = positions + TIME_STEP * fluid_mask[None] * new_vel
    moved = jnp.concatenate([new_pos, new_vel, density[None]], 0) * active[None]
    capacity = max(2, cell_count // (2 * peer_count))
    own_index = lax.axis_index("dev")
    group_owner = owners[0]
    own_owners = lax.dynamic_slice_in_dim(group_owner, own_index * cell_count, cell_count)
    one_hot = (own_owners[:, None] == jnp.arange(peer_count, dtype=jnp.int32)[None, :]).astype(
        jnp.int32
    )
    send_rank = jnp.sum((jnp.cumsum(one_hot, 0) - one_hot) * one_hot, 1)
    staying = own_owners == own_index
    slot_index = jnp.where(staying, peer_count * capacity, own_owners * capacity + send_rank)
    outbox = (
        jnp.zeros((7, peer_count * capacity, block_width), jnp.float32)
        .at[:, slot_index, :]
        .set(moved, mode="drop")
    )
    inbox = lax.all_to_all(outbox, "dev", split_axis=1, concat_axis=1, tiled=True)
    arrivals = jnp.sum(
        (group_owner.reshape(peer_count, cell_count) == own_index).astype(jnp.int32), 1
    )
    arrival_start = jnp.cumsum(arrivals) - arrivals
    rank_in = lax.broadcasted_iota(jnp.int32, (peer_count, capacity), 1)
    source_row = lax.broadcasted_iota(jnp.int32, (peer_count, capacity), 0)
    usable = (rank_in < arrivals[:, None]) & (source_row != own_index)
    arrival_slot = jnp.where(usable, arrival_start[:, None] + rank_in, cell_count).reshape(-1)
    keep_slot = jnp.where(staying, arrival_start[own_index] + send_rank, cell_count)
    settled = (
        jnp.zeros((7, cell_count, block_width), jnp.float32)
        .at[:, arrival_slot, :]
        .set(inbox, mode="drop")
    )
    settled = settled.at[:, keep_slot, :].set(moved, mode="drop")
    return (settled[0:6], settled[6])


def solution(mesh):
    return jax.shard_map(
        shards,
        mesh=mesh,
        in_specs=(
            P(None, ("group", "dev"), None),
            P(None, ("group", "dev"), None),
            P(("group", "dev"), None),
            P(("group", "dev")),
            P(("group", "dev"), None),
            P(("group", "dev"), None),
            P("group", "dev", None, None),
            P("group", None),
        ),
        out_specs=(P(None, ("group", "dev"), None), P(("group", "dev"), None)),
        check_vma=False,
    )
```

profile of v0, /device:TPU:0, one launch (start us, length us, event | category | flops | bytes accessed | tf_op | source)
XLA Modules:
  0.0 174.2 jit_solution(14094200770331152187)
XLA Ops:
  0.7 0.7 broadcast_maximum_fusion
  1.4 0.7 compare_convert_fusion.1
  2.1 0.9 multiply_bitcast_fusion.2
  3.0 1.0 copy.48
  4.9 0.7 multiply_bitcast_fusion.1
  5.7 5.2 %all-to-all-start = ((f32[4,16,256]{2,0,1:T(4,128)}), f32[4,16,256]{2,0,1:T(4,128)S(1)}, u32[]{:S(2)}, u32[]{:S(2)}) async-start(f32[4,16,256]{2,0,1:T(4,128)} %multiply_bitcast_fusion.1), calls=%async_computation | async-start | bytes 131072 | tf_op jit(solution)/shard_map/all_to_all | solution.py:102
  10.9 3.5 %collective-permute-start = (f32[4,4,256]{2,0,1:T(4,128)S(1)}, f32[4,4,256]{2,0,1:T(4,128)S(1)}, u32[]{:S(2)}, u32[]{:S(2)}) collective-permute-start(f32[4,4,256]{2,0,1:T(4,128)S(1)} %get-tuple-element.204), channel_id=1, source_target_pairs={{0,8},{8,16},{16,24},{1,9},{9,17},{17,25},{2,10},{10,18},{18,26},{... | collective-permute-start | bytes 49160 | tf_op jit(solution)/shard_map/ppermute | solution.py:25
  14.4 1.3 collective-permute-start.1
  16.6 0.6 dynamic_slice.14
  17.3 0.7 fusion.36
  18.3 1.7 collective-permute-done.1
  20.1 37.5 %while.20 = (s32[]{:T(128)}, f32[8,4,256]{2,1,0:T(4,128)S(1)}, s32[8,4]{1,0:T(8,128)S(1)}, s32[32,3]{1,0:T(8,128)S(1)}, f32[4,56,256]{2,0,1:T(4,128)S(1)}, /*index=5*/f32[3,32,256]{2,0,1:T(4,128)S(1)}, s32[]{:T(128)}) while((s32[]{:T(128)}, f32[8,4,256]{2,1,0:T(4,128)S(1)}, s32[8,4]{1,0:T(8,128)S(1)}, s32[32,3]{1,0:T(8,128)S(1)}, ...), condition=%wide.region_6.7_spmd, body=%wide.region_4.0_spmd.sunk | while | flops 15729746 | bytes 565941 | solution.py:110
  21.0 0.6 gather_fusion.1
  22.3 2.5 %fusion.57 = f32[4,256]{1,0:T(4,128)S(1)} fusion(f32[4,4,256]{2,1,0:T(4,128)S(1)} %get-tuple-element.339, f32[4,256]{1,0:T(4,128)S(1)} %get-tuple-element.342, f32[4,4,256]{2,1,0:T(4,128)S(1)} %get-tuple-element.343, f32[4,256]{1,0:T(4,128)S(1)} %get-tuple-element.344, f32[4,4,256]{2,1,0:T(4,128)S(1)} %get-tuple-element.347, ...), kind=kLoop, calls=%fused_computation.14.clone.1 | loop fusion | flops 15727616 | bytes 81920 | tf_op jit(solution)/shard_map/while/body/eval_jaxpr/reduce_sum | solution.py:43
  27.0 2.5 %fusion.57 = f32[4,256]{1,0:T(4,128)S(1)} fusion(f32[4,4,256]{2,1,0:T(4,128)S(1)} %get-tuple-element.339, f32[4,256]{1,0:T(4,128)S(1)} %get-tuple-element.342, f32[4,4,256]{2,1,0:T(4,128)S(1)} %get-tuple-element.343, f32[4,256]{1,0:T(4,128)S(1)} %get-tuple-element.344, f32[4,4,256]{2,1,0:T(4,128)S(1)} %get-tuple-element.347, ...), kind=kLoop, calls=%fused_computation.14.clone.1 | loop fusion | flops 15727616 | bytes 81920 | tf_op jit(solution)/shard_map/while/body/eval_jaxpr/reduce_sum | solution.py:43
  30.3 0.6 gather_fusion.1
  31.7 2.5 %fusion.57 = f32[4,256]{1,0:T(4,128)S(1)} fusion(f32[4,4,256]{2,1,0:T(4,128)S(1)} %get-tuple-element.339, f32[4,256]{1,0:T(4,128)S(1)} %get-tuple-element.342, f32[4,4,256]{2,1,0:T(4,128)S(1)} %get-tuple-element.343, f32[4,256]{1,0:T(4,128)S(1)} %get-tuple-element.344, f32[4,4,256]{2,1,0:T(4,128)S(1)} %get-tuple-element.347, ...), kind=kLoop, calls=%fused_computation.14.clone.1 | loop fusion | flops 15727616 | bytes 81920 | tf_op jit(solution)/shard_map/while/body/eval_jaxpr/reduce_sum | solution.py:43
  35.0 0.6 gather_fusion.1
  36.3 2.5 %fusion.57 = f32[4,256]{1,0:T(4,128)S(1)} fusion(f32[4,4,256]{2,1,0:T(4,128)S(1)} %get-tuple-element.339, f32[4,256]{1,0:T(4,128)S(1)} %get-tuple-element.342, f32[4,4,256]{2,1,0:T(4,128)S(1)} %get-tuple-element.343, f32[4,256]{1,0:T(4,128)S(1)} %get-tuple-element.344, f32[4,4,256]{2,1,0:T(4,128)S(1)} %get-tuple-element.347, ...), kind=kLoop, calls=%fused_computation.14.clone.1 | loop fusion | flops 15727616 | bytes 81920 | tf_op jit(solution)/shard_map/while/body/eval_jaxpr/reduce_sum | solution.py:43
  39.7 0.6 gather_fusion.1
  41.0 2.5 %fusion.57 = f32[4,256]{1,0:T(4,128)S(1)} fusion(f32[4,4,256]{2,1,0:T(4,128)S(1)} %get-tuple-element.339, f32[4,256]{1,0:T(4,128)S(1)} %get-tuple-element.342, f32[4,4,256]{2,1,0:T(4,128)S(1)} %get-tuple-element.343, f32[4,256]{1,0:T(4,128)S(1)} %get-tuple-element.344, f32[4,4,256]{2,1,0:T(4,128)S(1)} %get-tuple-element.347, ...), kind=kLoop, calls=%fused_computation.14.clone.1 | loop fusion | flops 15727616 | bytes 81920 | tf_op jit(solution)/shard_map/while/body/eval_jaxpr/reduce_sum | solution.py:43
  45.7 2.5 %fusion.57 = f32[4,256]{1,0:T(4,128)S(1)} fusion(f32[4,4,256]{2,1,0:T(4,128)S(1)} %get-tuple-element.339, f32[4,256]{1,0:T(4,128)S(1)} %get-tuple-element.342, f32[4,4,256]{2,1,0:T(4,128)S(1)} %get-tuple-element.343, f32[4,256]{1,0:T(4,128)S(1)} %get-tuple-element.344, f32[4,4,256]{2,1,0:T(4,128)S(1)} %get-tuple-element.347, ...), kind=kLoop, calls=%fused_computation.14.clone.1 | loop fusion | flops 15727616 | bytes 81920 | tf_op jit(solution)/shard_map/while/body/eval_jaxpr/reduce_sum | solution.py:43
  49.1 0.6 gather_fusion.1
  50.4 2.5 %fusion.57 = f32[4,256]{1,0:T(4,128)S(1)} fusion(f32[4,4,256]{2,1,0:T(4,128)S(1)} %get-tuple-element.339, f32[4,256]{1,0:T(4,128)S(1)} %get-tuple-element.342, f32[4,4,256]{2,1,0:T(4,128)S(1)} %get-tuple-element.343, f32[4,256]{1,0:T(4,128)S(1)} %get-tuple-element.344, f32[4,4,256]{2,1,0:T(4,128)S(1)} %get-tuple-element.347, ...), kind=kLoop, calls=%fused_computation.14.clone.1 | loop fusion | flops 15727616 | bytes 81920 | tf_op jit(solution)/shard_map/while/body/eval_jaxpr/reduce_sum | solution.py:43
  55.1 2.5 %fusion.57 = f32[4,256]{1,0:T(4,128)S(1)} fusion(f32[4,4,256]{2,1,0:T(4,128)S(1)} %get-tuple-element.339, f32[4,256]{1,0:T(4,128)S(1)} %get-tuple-element.342, f32[4,4,256]{2,1,0:T(4,128)S(1)} %get-tuple-element.343, f32[4,256]{1,0:T(4,128)S(1)} %get-tuple-element.344, f32[4,4,256]{2,1,0:T(4,128)S(1)} %get-tuple-element.347, ...), kind=kLoop, calls=%fused_computation.14.clone.1 | loop fusion | flops 15727616 | bytes 81920 | tf_op jit(solution)/shard_map/while/body/eval_jaxpr/reduce_sum | solution.py:43
  58.7 0.8 multiply_bitcast_fusion
  59.5 4.2 %all-to-all-start.1 = ((f32[9,16,256]{2,0,1:T(8,128)}), f32[9,16,256]{2,0,1:T(8,128)S(1)}, u32[]{:S(2)}, u32[]{:S(2)}) async-start(f32[9,16,256]{2,0,1:T(8,128)} %multiply_bitcast_fusion), calls=%async_computation.1 | async-start | bytes 524288 | tf_op jit(solution)/shard_map/all_to_all | solution.py:118
  63.7 3.5 %collective-permute-start.2 = (f32[9,4,256]{2,0,1:T(8,128)S(1)}, f32[9,4,256]{2,0,1:T(8,128)S(1)}, u32[]{:S(2)}, u32[]{:S(2)}) collective-permute-start(f32[9,4,256]{2,0,1:T(8,128)S(1)} %get-tuple-element.202), channel_id=1, source_target_pairs={{0,8},{8,16},{16,24},{1,9},{9,17},{17,25},{2,10},{10,18},{18,26},{... | collective-permute-start | bytes 110600 | tf_op jit(solution)/shard_map/ppermute | solution.py:25
  67.2 1.3 collective-permute-start.3
  68.6 0.6 collective-permute-done.2
  69.2 4.2 %collective-permute-done.3 = f32[9,4,256]{2,0,1:T(8,128)S(1)} collective-permute-done((f32[9,4,256]{2,0,1:T(8,128)S(1)}, f32[9,4,256]{2,0,1:T(8,128)S(1)}, u32[]{:S(2)}, u32[]{:S(2)}) %collective-permute-start.3) | collective-permute-done | bytes 36896 | tf_op jit(solution)/shard_map/ppermute | solution.py:27
  73.5 81.7 %while.21 = (s32[]{:T(128)}, f32[8,3,4,256]{3,1,2,0:T(4,128)S(1)}, s32[8,4]{1,0:T(8,128)S(1)}, f32[3,32,256]{2,0,1:T(4,128)S(1)}, s32[32,3]{1,0:T(8,128)S(1)}, /...) while((s32[]{:T(128)}, f32[8,3,4,256]{3,1,2,0:T(4,128)S(1)}, ...), condition=%wide.region_12.13_spmd, body=%wide.region_7.12_spmd.sunk | while | flops 35666000 | bytes 1299173 | solution.py:131
  76.3 6.7 %fusion.61 = (f32[4,256]{1,0:T(4,128)S(1)}, f32[4,256]{1,0:T(4,128)S(1)}, f32[4,256]{1,0:T(4,128)S(1)}, f32[4,256]{1,0:T(4,128)S(1)}) fusion(f32[4,4,256]{2,1,0:T(4,128)S(1)} %get-tuple-element.362, f32[4,4,256]{2,1,0:T(4,128)S(1)} %bitcast.193, f32[4,256]{1,0:T(4,128)S(1)} %bitcast.198, f32[4,4,256]{2,1,0:T(4,128)S(1)} %get-tuple-element.367, ...), kind=kLoop, calls=%fused_computation.45.clone.1 | loop fusion | flops 35647488 | bytes 196608 | tf_op jit(solution)/shard_map/while/body/eval_jaxpr/reduce_sum | solution.py:71
  86.5 6.7 %fusion.61 = (f32[4,256]{1,0:T(4,128)S(1)}, f32[4,256]{1,0:T(4,128)S(1)}, f32[4,256]{1,0:T(4,128)S(1)}, f32[4,256]{1,0:T(4,128)S(1)}) fusion(f32[4,4,256]{2,1,0:T(4,128)S(1)} %get-tuple-element.362, f32[4,4,256]{2,1,0:T(4,128)S(1)} %bitcast.193, f32[4,256]{1,0:T(4,128)S(1)} %bitcast.198, f32[4,4,256]{2,1,0:T(4,128)S(1)} %get-tuple-element.367, ...), kind=kLoop, calls=%fused_computation.45.clone.1 | loop fusion | flops 35647488 | bytes 196608 | tf_op jit(solution)/shard_map/while/body/eval_jaxpr/reduce_sum | solution.py:71
  96.7 6.7 %fusion.61 = (f32[4,256]{1,0:T(4,128)S(1)}, f32[4,256]{1,0:T(4,128)S(1)}, f32[4,256]{1,0:T(4,128)S(1)}, f32[4,256]{1,0:T(4,128)S(1)}) fusion(f32[4,4,256]{2,1,0:T(4,128)S(1)} %get-tuple-element.362, f32[4,4,256]{2,1,0:T(4,128)S(1)} %bitcast.193, f32[4,256]{1,0:T(4,128)S(1)} %bitcast.198, f32[4,4,256]{2,1,0:T(4,128)S(1)} %get-tuple-element.367, ...), kind=kLoop, calls=%fused_computation.45.clone.1 | loop fusion | flops 35647488 | bytes 196608 | tf_op jit(solution)/shard_map/while/body/eval_jaxpr/reduce_sum | solution.py:71
  106.9 6.7 %fusion.61 = (f32[4,256]{1,0:T(4,128)S(1)}, f32[4,256]{1,0:T(4,128)S(1)}, f32[4,256]{1,0:T(4,128)S(1)}, f32[4,256]{1,0:T(4,128)S(1)}) fusion(f32[4,4,256]{2,1,0:T(4,128)S(1)} %get-tuple-element.362, f32[4,4,256]{2,1,0:T(4,128)S(1)} %bitcast.193, f32[4,256]{1,0:T(4,128)S(1)} %bitcast.198, f32[4,4,256]{2,1,0:T(4,128)S(1)} %get-tuple-element.367, ...), kind=kLoop, calls=%fused_computation.45.clone.1 | loop fusion | flops 35647488 | bytes 196608 | tf_op jit(solution)/shard_map/while/body/eval_jaxpr/reduce_sum | solution.py:71
  117.2 6.7 %fusion.61 = (f32[4,256]{1,0:T(4,128)S(1)}, f32[4,256]{1,0:T(4,128)S(1)}, f32[4,256]{1,0:T(4,128)S(1)}, f32[4,256]{1,0:T(4,128)S(1)}) fusion(f32[4,4,256]{2,1,0:T(4,128)S(1)} %get-tuple-element.362, f32[4,4,256]{2,1,0:T(4,128)S(1)} %bitcast.193, f32[4,256]{1,0:T(4,128)S(1)} %bitcast.198, f32[4,4,256]{2,1,0:T(4,128)S(1)} %get-tuple-element.367, ...), kind=kLoop, calls=%fused_computation.45.clone.1 | loop fusion | flops 35647488 | bytes 196608 | tf_op jit(solution)/shard_map/while/body/eval_jaxpr/reduce_sum | solution.py:71
  127.4 6.7 %fusion.61 = (f32[4,256]{1,0:T(4,128)S(1)}, f32[4,256]{1,0:T(4,128)S(1)}, f32[4,256]{1,0:T(4,128)S(1)}, f32[4,256]{1,0:T(4,128)S(1)}) fusion(f32[4,4,256]{2,1,0:T(4,128)S(1)} %get-tuple-element.362, f32[4,4,256]{2,1,0:T(4,128)S(1)} %bitcast.193, f32[4,256]{1,0:T(4,128)S(1)} %bitcast.198, f32[4,4,256]{2,1,0:T(4,128)S(1)} %get-tuple-element.367, ...), kind=kLoop, calls=%fused_computation.45.clone.1 | loop fusion | flops 35647488 | bytes 196608 | tf_op jit(solution)/shard_map/while/body/eval_jaxpr/reduce_sum | solution.py:71
  137.6 6.7 %fusion.61 = (f32[4,256]{1,0:T(4,128)S(1)}, f32[4,256]{1,0:T(4,128)S(1)}, f32[4,256]{1,0:T(4,128)S(1)}, f32[4,256]{1,0:T(4,128)S(1)}) fusion(f32[4,4,256]{2,1,0:T(4,128)S(1)} %get-tuple-element.362, f32[4,4,256]{2,1,0:T(4,128)S(1)} %bitcast.193, f32[4,256]{1,0:T(4,128)S(1)} %bitcast.198, f32[4,4,256]{2,1,0:T(4,128)S(1)} %get-tuple-element.367, ...), kind=kLoop, calls=%fused_computation.45.clone.1 | loop fusion | flops 35647488 | bytes 196608 | tf_op jit(solution)/shard_map/while/body/eval_jaxpr/reduce_sum | solution.py:71
  147.8 6.7 %fusion.61 = (f32[4,256]{1,0:T(4,128)S(1)}, f32[4,256]{1,0:T(4,128)S(1)}, f32[4,256]{1,0:T(4,128)S(1)}, f32[4,256]{1,0:T(4,128)S(1)}) fusion(f32[4,4,256]{2,1,0:T(4,128)S(1)} %get-tuple-element.362, f32[4,4,256]{2,1,0:T(4,128)S(1)} %bitcast.193, f32[4,256]{1,0:T(4,128)S(1)} %bitcast.198, f32[4,4,256]{2,1,0:T(4,128)S(1)} %get-tuple-element.367, ...), kind=kLoop, calls=%fused_computation.45.clone.1 | loop fusion | flops 35647488 | bytes 196608 | tf_op jit(solution)/shard_map/while/body/eval_jaxpr/reduce_sum | solution.py:71
  155.5 0.7 broadcast_in_dim.48
  156.2 4.3 %scatter_fusion = f32[7,16,256]{2,0,1:T(8,128)} fusion(f32[7,16,256]{2,0,1:T(8,128)} %broadcast_in_dim.48, s32[32]{0:T(128)S(1)} %get-tuple-element.210, f32[32,7,256]{2,1,0:T(8,128)S(1)} %copy.53), kind=kCustom, calls=%fused_computation.10 | custom fusion | bytes 688256 | tf_op jit(solution)/shard_map/scatter | solution.py:151
  160.5 4.2 %all-to-all-start.2 = ((f32[7,16,256]{2,0,1:T(8,128)}), f32[7,16,256]{2,0,1:T(8,128)S(1)}, u32[]{:S(2)}, u32[]{:S(2)}) async-start(f32[7,16,256]{2,0,1:T(8,128)} %scatter_fusion), calls=%async_computation.2 | async-start | bytes 262144 | tf_op jit(solution)/shard_map/all_to_all | solution.py:153
  164.7 5.5 %all-to-all-done.2 = f32[7,16,256]{2,0,1:T(8,128)S(1)} async-done(((f32[7,16,256]{2,0,1:T(8,128)}), f32[7,16,256]{2,0,1:T(8,128)S(1)}, u32[]{:S(2)}, u32[]{:S(2)}) %all-to-all-start.2) | async-done | bytes 114720 | tf_op jit(solution)/shard_map/all_to_all | solution.py:153
  170.2 1.0 scatter_fusion.1
  171.3 1.5 scatter_fusion.2
  172.8 0.7 copy.55
  173.5 0.6 copy.108
  (366 shorter events, 44.5 us)
Async XLA Ops:
  0.6 15.0 %copy-start.2 = (s32[32]{0:T(128)S(1)}, s32[32]{0:T(128)}, u32[]{:S(2)}) copy-start(s32[32]{0:T(128)} %param.16) | copy-start | bytes 388
  0.6 15.1 %copy-start.3 = (s32[1,256]{1,0:T(1,128)S(1)}, s32[1,256]{1,0:T(1,128)}, u32[]{:S(2)}) copy-start(s32[1,256]{1,0:T(1,128)} %param.20) | copy-start | bytes 3076
  0.7 17.3 %copy-start.4 = (s32[32,3]{0,1:T(4,128)S(1)}, s32[32,3]{0,1:T(4,128)}, u32[]{:S(2)}) copy-start(s32[32,3]{0,1:T(4,128)} %param.18) | copy-start | bytes 1156
  0.7 17.4 %copy-start.1 = (f32[3,32,256]{2,1,0:T(8,128)S(1)}, f32[3,32,256]{2,1,0:T(8,128)}, u32[]{:S(2)}) copy-start(f32[3,32,256]{2,1,0:T(8,128)} %param.14) | copy-start | bytes 294916
  5.7 14.3 %all-to-all-start = ((f32[4,16,256]{2,0,1:T(4,128)}), f32[4,16,256]{2,0,1:T(4,128)S(1)}, u32[]{:S(2)}, u32[]{:S(2)}) async-start(f32[4,16,256]{2,0,1:T(4,128)} %multiply_bitcast_fusion.1), calls=%async_computation | async-start | bytes 131072 | tf_op jit(solution)/shard_map/all_to_all | solution.py:102
  10.9 7.4 %collective-permute-start = (f32[4,4,256]{2,0,1:T(4,128)S(1)}, f32[4,4,256]{2,0,1:T(4,128)S(1)}, u32[]{:S(2)}, u32[]{:S(2)}) collective-permute-start(f32[4,4,256]{2,0,1:T(4,128)S(1)} %get-tuple-element.204), channel_id=1, source_target_pairs={{0,8},{8,16},{16,24},{1,9},{9,17},{17,25},{2,10},{10,18},{18,26},{... | collective-permute-start | bytes 49160 | tf_op jit(solution)/shard_map/ppermute | solution.py:25
  14.4 5.6 %collective-permute-start.1 = (f32[4,4,256]{2,0,1:T(4,128)S(1)}, f32[4,4,256]{2,0,1:T(4,128)S(1)}, u32[]{:S(2)}, u32[]{:S(2)}) collective-permute-start(f32[4,4,256]{2,0,1:T(4,128)S(1)} %get-tuple-element.205), channel_id=1, source_target_pairs={{8,0},{16,8},{24,16},{9,1},{17,9},{25,17},{10,2},{18,10},{26,18},{... | collective-permute-start | bytes 49160 | tf_op jit(solution)/shard_map/ppermute | solution.py:27
  59.5 13.8 %all-to-all-start.1 = ((f32[9,16,256]{2,0,1:T(8,128)}), f32[9,16,256]{2,0,1:T(8,128)S(1)}, u32[]{:S(2)}, u32[]{:S(2)}) async-start(f32[9,16,256]{2,0,1:T(8,128)} %multiply_bitcast_fusion), calls=%async_computation.1 | async-start | bytes 524288 | tf_op jit(solution)/shard_map/all_to_all | solution.py:118
  63.7 5.5 %collective-permute-start.2 = (f32[9,4,256]{2,0,1:T(8,128)S(1)}, f32[9,4,256]{2,0,1:T(8,128)S(1)}, u32[]{:S(2)}, u32[]{:S(2)}) collective-permute-start(f32[9,4,256]{2,0,1:T(8,128)S(1)} %get-tuple-element.202), channel_id=1, source_target_pairs={{0,8},{8,16},{16,24},{1,9},{9,17},{17,25},{2,10},{10,18},{18,26},{... | collective-permute-start | bytes 110600 | tf_op jit(solution)/shard_map/ppermute | solution.py:25
  67.2 6.2 %collective-permute-start.3 = (f32[9,4,256]{2,0,1:T(8,128)S(1)}, f32[9,4,256]{2,0,1:T(8,128)S(1)}, u32[]{:S(2)}, u32[]{:S(2)}) collective-permute-start(f32[9,4,256]{2,0,1:T(8,128)S(1)} %get-tuple-element.203), channel_id=1, source_target_pairs={{8,0},{16,8},{24,16},{9,1},{17,9},{25,17},{10,2},{18,10},{26,18},{... | collective-permute-start | bytes 110600 | tf_op jit(solution)/shard_map/ppermute | solution.py:27
  73.4 81.8 %copy-start = (f32[3,32,256]{2,1,0:T(8,128)S(1)}, f32[3,32,256]{2,1,0:T(8,128)}, u32[]{:S(2)}) copy-start(f32[3,32,256]{2,1,0:T(8,128)} %param.13) | copy-start | bytes 294916
  73.4 81.8 %copy-start.5 = (f32[3]{0:T(128)S(1)}, f32[3]{0:T(128)}, u32[]{:S(2)}) copy-start(f32[3]{0:T(128)} %constant.111) | copy-start | bytes 40
  160.5 9.7 %all-to-all-start.2 = ((f32[7,16,256]{2,0,1:T(8,128)}), f32[7,16,256]{2,0,1:T(8,128)S(1)}, u32[]{:S(2)}, u32[]{:S(2)}) async-start(f32[7,16,256]{2,0,1:T(8,128)} %scatter_fusion), calls=%async_computation.2 | async-start | bytes 262144 | tf_op jit(solution)/shard_map/all_to_all | solution.py:153
where the time goes:
time: 175 us; the launch traced here: 174 us
  other arithmetic  81.9 us (47%)
  local copies, waits for them, and re-layouts  54.5 us (31%)
  starting transfers between devices  23.1 us (13%)
  waiting for transfers between devices  12 us (7%)
  loops' own time  1.75 us (1%)
    reduce_sum x8, other arithmetic, pair_force(): jnp.sum(offsets[component] * pushes + damping * remote[3 + component][:,...  54 us
    reduce_sum x8, other arithmetic, pair_density(): jnp.sum(remote[3][:, None, :, :] * weight * weight * weight, axis=(2, 3))  20 us
    ppermute x2, starting transfers between devices, with_halo(): lax.ppermute(tail, axis, [(i, (i + 1) % count) for i in range(ends)])  6.96 us
    ppermute x2, waiting for transfers between devices, with_halo(): lax.ppermute(head, axis, [((i + 1) % count, i) for i in range(ends)])  5.9 us
    all_to_all x1, waiting for transfers between devices, shards(): lax.all_to_all(outbox, 'dev', split_axis=1, concat_axis=1, tiled=True)  5.49 us
    all_to_all x1, starting transfers between devices, shards(): lax.all_to_all(outgoing(dens_field), 'dev', split_axis=1, concat_axis=1,...  5.2 us
    gather x8, local copies, waits for them, and re-layouts, pair_density(): remote = lookup[:, columns, :]  4.75 us
    gather x8, local copies, waits for them, and re-layouts, force_block(): velocities[:, cell_ids, :]  4.59 us
  transfers between devices with their start and end apart: 7, of which 4 were waited for; matrix products, arithmetic and copies ran while one was open for 2% of the time, Pallas kernels for 0%

commit v1 on v0

--- a/solution.py
+++ b/solution.py
@@ -150,7 +150,19 @@
         .at[:, slot_index, :]
         .set(moved, mode="drop")
     )
-    inbox = lax.all_to_all(outbox, "dev", split_axis=1, concat_axis=1, tiled=True)
+    ways, here = (lax.axis_size("dev"), lax.axis_index("dev"))
+    width_2 = outbox.shape[1] // ways
+    dims = list(outbox.shape)
+    dims[1] = width_2
+    height = dims[1]
+    dims[1] = height * ways
+    full = jnp.zeros(dims, outbox.dtype)
+    for mask in range(ways):
+        part = lax.dynamic_slice_in_dim(outbox, (here ^ mask) * width_2, width_2, axis=1)
+        if mask:
+            part = lax.ppermute(part, "dev", [(d, d ^ mask) for d in range(ways)])
+        full = lax.dynamic_update_slice_in_dim(full, part, (here ^ mask) * height, axis=1)
+    inbox = full
     arrivals = jnp.sum(
         (group_owner.reshape(peer_count, cell_count) == own_index).astype(jnp.int32), 1
     )

time: 175 us -> 172 us (0.983)
  local copies, waits for them, and re-layouts: 54.5 us -> 51.1 us
  starting transfers between devices: 23.1 us -> 25.6 us
    ppermute x0 -> x7, starting transfers between devices: none -> 6.66 us  [shards(): part = lax.ppermute(part, 'dev', [(d, d ^ mask) for d in range(ways)])]
    all_to_all x1 -> x0, waiting for transfers between devices: 5.49 us -> none  [shards(): lax.all_to_all(outbox, 'dev', split_axis=1, concat_axis=1, tiled=True)]
    all_to_all x1 -> x0, starting transfers between devices: 4.18 us -> none  [shards(): lax.all_to_all(outbox, 'dev', split_axis=1, concat_axis=1, tiled=True)]
    ppermute x0 -> x7, waiting for transfers between devices: none -> 3.92 us  [shards(): part = lax.ppermute(part, 'dev', [(d, d ^ mask) for d in range(ways)])]
    scatter x1, local copies, waits for them, and re-layouts: 4.34 us -> 1.56 us  [shards(): outbox = jnp.zeros((7, peer_count * capacity, block_width), jnp.float32)....]
  transfers between devices with their start and end apart: 7 -> 13, of which waited for: 4 -> 6; matrix products, arithmetic and copies ran while one was open for 2% -> 2% of each run, Pallas kernels for 0% -> 0%
where the time goes in v1:
time: 172 us
  other arithmetic  81.9 us (48%)
  local copies, waits for them, and re-layouts  51.1 us (30%)
  starting transfers between devices  25.6 us (15%)
  waiting for transfers between devices  10.4 us (6%)
  loops' own time  1.75 us (1%)
    reduce_sum x8, other arithmetic, pair_force(): jnp.sum(offsets[component] * pushes + damping * remote[3 + component][:,...  54 us
    reduce_sum x8, other arithmetic, pair_density(): jnp.sum(remote[3][:, None, :, :] * weight * weight * weight, axis=(2, 3))  20 us
    ppermute x2, starting transfers between devices, with_halo(): lax.ppermute(tail, axis, [(i, (i + 1) % count) for i in range(ends)])  6.96 us
    ppermute x7, starting transfers between devices, shards(): part = lax.ppermute(part, 'dev', [(d, d ^ mask) for d in range(ways)])  6.66 us
    ppermute x2, waiting for transfers between devices, with_halo(): lax.ppermute(head, axis, [((i + 1) % count, i) for i in range(ends)])  5.83 us
    all_to_all x1, starting transfers between devices, shards(): lax.all_to_all(outgoing(dens_field), 'dev', split_axis=1, concat_axis=1,...  5.2 us
    gather x8, local copies, waits for them, and re-layouts, pair_density(): remote = lookup[:, columns, :]  4.75 us
    gather x8, local copies, waits for them, and re-layouts, force_block(): velocities[:, cell_ids, :]  4.59 us
  transfers between devices with their start and end apart: 13, of which 6 were waited for; matrix products, arithmetic and copies ran while one was open for 2% of the time, Pallas kernels for 0%

profile of v1, /device:TPU:0, one launch (start us, length us, event | category | flops | bytes accessed | tf_op | source)
XLA Modules:
  0.0 171.8 jit_solution(12682704590440829815)
XLA Ops:
  0.7 0.7 broadcast_maximum_fusion
  1.4 0.7 compare_convert_fusion.1
  2.1 0.9 multiply_bitcast_fusion.2
  3.0 1.0 copy.48
  4.9 0.7 multiply_bitcast_fusion.1
  5.7 5.2 %all-to-all-start = ((f32[4,16,256]{2,0,1:T(4,128)}), f32[4,16,256]{2,0,1:T(4,128)S(1)}, u32[]{:S(2)}, u32[]{:S(2)}) async-start(f32[4,16,256]{2,0,1:T(4,128)} %multiply_bitcast_fusion.1), calls=%async_computation | async-start | bytes 131072 | tf_op jit(solution)/shard_map/all_to_all | solution.py:102
  10.9 3.5 %collective-permute-start = (f32[4,4,256]{2,0,1:T(4,128)S(1)}, f32[4,4,256]{2,0,1:T(4,128)S(1)}, u32[]{:S(2)}, u32[]{:S(2)}) collective-permute-start(f32[4,4,256]{2,0,1:T(4,128)S(1)} %get-tuple-element.204), channel_id=1, source_target_pairs={{0,8},{8,16},{16,24},{1,9},{9,17},{17,25},{2,10},{10,18},{18,26},{... | collective-permute-start | bytes 49160 | tf_op jit(solution)/shard_map/ppermute | solution.py:25
  14.4 1.3 collective-permute-start.1
  16.6 0.6 dynamic_slice.46
  17.3 0.7 fusion.36
  18.3 1.7 collective-permute-done.1
  20.1 37.5 %while.20 = (s32[]{:T(128)}, f32[8,4,256]{2,1,0:T(4,128)S(1)}, s32[8,4]{1,0:T(8,128)S(1)}, s32[32,3]{1,0:T(8,128)S(1)}, f32[4,56,256]{2,0,1:T(4,128)S(1)}, /*index=5*/f32[3,32,256]{2,0,1:T(4,128)S(1)}, s32[]{:T(128)}) while((s32[]{:T(128)}, f32[8,4,256]{2,1,0:T(4,128)S(1)}, s32[8,4]{1,0:T(8,128)S(1)}, s32[32,3]{1,0:T(8,128)S(1)}, ...), condition=%wide.region_6.7_spmd, body=%wide.region_4.0_spmd.sunk | while | flops 15729746 | bytes 565941 | solution.py:110
  22.3 2.5 %fusion.57 = f32[4,256]{1,0:T(4,128)S(1)} fusion(f32[4,4,256]{2,1,0:T(4,128)S(1)} %get-tuple-element.347, f32[4,256]{1,0:T(4,128)S(1)} %get-tuple-element.350, f32[4,4,256]{2,1,0:T(4,128)S(1)} %get-tuple-element.351, f32[4,256]{1,0:T(4,128)S(1)} %get-tuple-element.352, f32[4,4,256]{2,1,0:T(4,128)S(1)} %get-tuple-element.355, ...), kind=kLoop, calls=%fused_computation.14.clone.1 | loop fusion | flops 15727616 | bytes 81920 | tf_op jit(solution)/shard_map/while/body/eval_jaxpr/reduce_sum | solution.py:43
  27.0 2.5 %fusion.57 = f32[4,256]{1,0:T(4,128)S(1)} fusion(f32[4,4,256]{2,1,0:T(4,128)S(1)} %get-tuple-element.347, f32[4,256]{1,0:T(4,128)S(1)} %get-tuple-element.350, f32[4,4,256]{2,1,0:T(4,128)S(1)} %get-tuple-element.351, f32[4,256]{1,0:T(4,128)S(1)} %get-tuple-element.352, f32[4,4,256]{2,1,0:T(4,128)S(1)} %get-tuple-element.355, ...), kind=kLoop, calls=%fused_computation.14.clone.1 | loop fusion | flops 15727616 | bytes 81920 | tf_op jit(solution)/shard_map/while/body/eval_jaxpr/reduce_sum | solution.py:43
  30.3 0.6 gather_fusion.1
  31.7 2.5 %fusion.57 = f32[4,256]{1,0:T(4,128)S(1)} fusion(f32[4,4,256]{2,1,0:T(4,128)S(1)} %get-tuple-element.347, f32[4,256]{1,0:T(4,128)S(1)} %get-tuple-element.350, f32[4,4,256]{2,1,0:T(4,128)S(1)} %get-tuple-element.351, f32[4,256]{1,0:T(4,128)S(1)} %get-tuple-element.352, f32[4,4,256]{2,1,0:T(4,128)S(1)} %get-tuple-element.355, ...), kind=kLoop, calls=%fused_computation.14.clone.1 | loop fusion | flops 15727616 | bytes 81920 | tf_op jit(solution)/shard_map/while/body/eval_jaxpr/reduce_sum | solution.py:43
  36.3 2.5 %fusion.57 = f32[4,256]{1,0:T(4,128)S(1)} fusion(f32[4,4,256]{2,1,0:T(4,128)S(1)} %get-tuple-element.347, f32[4,256]{1,0:T(4,128)S(1)} %get-tuple-element.350, f32[4,4,256]{2,1,0:T(4,128)S(1)} %get-tuple-element.351, f32[4,256]{1,0:T(4,128)S(1)} %get-tuple-element.352, f32[4,4,256]{2,1,0:T(4,128)S(1)} %get-tuple-element.355, ...), kind=kLoop, calls=%fused_computation.14.clone.1 | loop fusion | flops 15727616 | bytes 81920 | tf_op jit(solution)/shard_map/while/body/eval_jaxpr/reduce_sum | solution.py:43
  39.7 0.6 gather_fusion.1
  41.0 2.5 %fusion.57 = f32[4,256]{1,0:T(4,128)S(1)} fusion(f32[4,4,256]{2,1,0:T(4,128)S(1)} %get-tuple-element.347, f32[4,256]{1,0:T(4,128)S(1)} %get-tuple-element.350, f32[4,4,256]{2,1,0:T(4,128)S(1)} %get-tuple-element.351, f32[4,256]{1,0:T(4,128)S(1)} %get-tuple-element.352, f32[4,4,256]{2,1,0:T(4,128)S(1)} %get-tuple-element.355, ...), kind=kLoop, calls=%fused_computation.14.clone.1 | loop fusion | flops 15727616 | bytes 81920 | tf_op jit(solution)/shard_map/while/body/eval_jaxpr/reduce_sum | solution.py:43
  45.7 2.5 %fusion.57 = f32[4,256]{1,0:T(4,128)S(1)} fusion(f32[4,4,256]{2,1,0:T(4,128)S(1)} %get-tuple-element.347, f32[4,256]{1,0:T(4,128)S(1)} %get-tuple-element.350, f32[4,4,256]{2,1,0:T(4,128)S(1)} %get-tuple-element.351, f32[4,256]{1,0:T(4,128)S(1)} %get-tuple-element.352, f32[4,4,256]{2,1,0:T(4,128)S(1)} %get-tuple-element.355, ...), kind=kLoop, calls=%fused_computation.14.clone.1 | loop fusion | flops 15727616 | bytes 81920 | tf_op jit(solution)/shard_map/while/body/eval_jaxpr/reduce_sum | solution.py:43
  49.1 0.6 gather_fusion.1
  50.4 2.5 %fusion.57 = f32[4,256]{1,0:T(4,128)S(1)} fusion(f32[4,4,256]{2,1,0:T(4,128)S(1)} %get-tuple-element.347, f32[4,256]{1,0:T(4,128)S(1)} %get-tuple-element.350, f32[4,4,256]{2,1,0:T(4,128)S(1)} %get-tuple-element.351, f32[4,256]{1,0:T(4,128)S(1)} %get-tuple-element.352, f32[4,4,256]{2,1,0:T(4,128)S(1)} %get-tuple-element.355, ...), kind=kLoop, calls=%fused_computation.14.clone.1 | loop fusion | flops 15727616 | bytes 81920 | tf_op jit(solution)/shard_map/while/body/eval_jaxpr/reduce_sum | solution.py:43
  55.1 2.5 %fusion.57 = f32[4,256]{1,0:T(4,128)S(1)} fusion(f32[4,4,256]{2,1,0:T(4,128)S(1)} %get-tuple-element.347, f32[4,256]{1,0:T(4,128)S(1)} %get-tuple-element.350, f32[4,4,256]{2,1,0:T(4,128)S(1)} %get-tuple-element.351, f32[4,256]{1,0:T(4,128)S(1)} %get-tuple-element.352, f32[4,4,256]{2,1,0:T(4,128)S(1)} %get-tuple-element.355, ...), kind=kLoop, calls=%fused_computation.14.clone.1 | loop fusion | flops 15727616 | bytes 81920 | tf_op jit(solution)/shard_map/while/body/eval_jaxpr/reduce_sum | solution.py:43
  58.7 0.8 multiply_bitcast_fusion
  59.5 4.2 %all-to-all-start.1 = ((f32[9,16,256]{2,0,1:T(8,128)}), f32[9,16,256]{2,0,1:T(8,128)S(1)}, u32[]{:S(2)}, u32[]{:S(2)}) async-start(f32[9,16,256]{2,0,1:T(8,128)} %multiply_bitcast_fusion), calls=%async_computation.1 | async-start | bytes 524288 | tf_op jit(solution)/shard_map/all_to_all | solution.py:118
  63.7 3.5 %collective-permute-start.2 = (f32[9,4,256]{2,0,1:T(8,128)S(1)}, f32[9,4,256]{2,0,1:T(8,128)S(1)}, u32[]{:S(2)}, u32[]{:S(2)}) collective-permute-start(f32[9,4,256]{2,0,1:T(8,128)S(1)} %get-tuple-element.202), channel_id=1, source_target_pairs={{0,8},{8,16},{16,24},{1,9},{9,17},{17,25},{2,10},{10,18},{18,26},{... | collective-permute-start | bytes 110600 | tf_op jit(solution)/shard_map/ppermute | solution.py:25
  67.2 1.3 collective-permute-start.3
  68.6 0.6 collective-permute-done.2
  69.2 4.2 %collective-permute-done.3 = f32[9,4,256]{2,0,1:T(8,128)S(1)} collective-permute-done((f32[9,4,256]{2,0,1:T(8,128)S(1)}, f32[9,4,256]{2,0,1:T(8,128)S(1)}, u32[]{:S(2)}, u32[]{:S(2)}) %collective-permute-start.3) | collective-permute-done | bytes 36896 | tf_op jit(solution)/shard_map/ppermute | solution.py:27
  73.5 81.7 %while.21 = (s32[]{:T(128)}, f32[8,3,4,256]{3,1,2,0:T(4,128)S(1)}, s32[8,4]{1,0:T(8,128)S(1)}, f32[3,32,256]{2,0,1:T(4,128)S(1)}, s32[32,3]{1,0:T(8,128)S(1)}, /...) while((s32[]{:T(128)}, f32[8,3,4,256]{3,1,2,0:T(4,128)S(1)}, ...), condition=%wide.region_12.13_spmd, body=%wide.region_7.12_spmd.sunk | while | flops 35666000 | bytes 1299173 | solution.py:131
  76.3 6.7 %fusion.61 = (f32[4,256]{1,0:T(4,128)S(1)}, f32[4,256]{1,0:T(4,128)S(1)}, f32[4,256]{1,0:T(4,128)S(1)}, f32[4,256]{1,0:T(4,128)S(1)}) fusion(f32[4,4,256]{2,1,0:T(4,128)S(1)} %get-tuple-element.370, f32[4,4,256]{2,1,0:T(4,128)S(1)} %bitcast.193, f32[4,256]{1,0:T(4,128)S(1)} %bitcast.198, f32[4,4,256]{2,1,0:T(4,128)S(1)} %get-tuple-element.375, ...), kind=kLoop, calls=%fused_computation.45.clone.1 | loop fusion | flops 35647488 | bytes 196608 | tf_op jit(solution)/shard_map/while/body/eval_jaxpr/reduce_sum | solution.py:71
  86.5 6.7 %fusion.61 = (f32[4,256]{1,0:T(4,128)S(1)}, f32[4,256]{1,0:T(4,128)S(1)}, f32[4,256]{1,0:T(4,128)S(1)}, f32[4,256]{1,0:T(4,128)S(1)}) fusion(f32[4,4,256]{2,1,0:T(4,128)S(1)} %get-tuple-element.370, f32[4,4,256]{2,1,0:T(4,128)S(1)} %bitcast.193, f32[4,256]{1,0:T(4,128)S(1)} %bitcast.198, f32[4,4,256]{2,1,0:T(4,128)S(1)} %get-tuple-element.375, ...), kind=kLoop, calls=%fused_computation.45.clone.1 | loop fusion | flops 35647488 | bytes 196608 | tf_op jit(solution)/shard_map/while/body/eval_jaxpr/reduce_sum | solution.py:71
  96.7 6.7 %fusion.61 = (f32[4,256]{1,0:T(4,128)S(1)}, f32[4,256]{1,0:T(4,128)S(1)}, f32[4,256]{1,0:T(4,128)S(1)}, f32[4,256]{1,0:T(4,128)S(1)}) fusion(f32[4,4,256]{2,1,0:T(4,128)S(1)} %get-tuple-element.370, f32[4,4,256]{2,1,0:T(4,128)S(1)} %bitcast.193, f32[4,256]{1,0:T(4,128)S(1)} %bitcast.198, f32[4,4,256]{2,1,0:T(4,128)S(1)} %get-tuple-element.375, ...), kind=kLoop, calls=%fused_computation.45.clone.1 | loop fusion | flops 35647488 | bytes 196608 | tf_op jit(solution)/shard_map/while/body/eval_jaxpr/reduce_sum | solution.py:71
  106.9 6.7 %fusion.61 = (f32[4,256]{1,0:T(4,128)S(1)}, f32[4,256]{1,0:T(4,128)S(1)}, f32[4,256]{1,0:T(4,128)S(1)}, f32[4,256]{1,0:T(4,128)S(1)}) fusion(f32[4,4,256]{2,1,0:T(4,128)S(1)} %get-tuple-element.370, f32[4,4,256]{2,1,0:T(4,128)S(1)} %bitcast.193, f32[4,256]{1,0:T(4,128)S(1)} %bitcast.198, f32[4,4,256]{2,1,0:T(4,128)S(1)} %get-tuple-element.375, ...), kind=kLoop, calls=%fused_computation.45.clone.1 | loop fusion | flops 35647488 | bytes 196608 | tf_op jit(solution)/shard_map/while/body/eval_jaxpr/reduce_sum | solution.py:71
  117.2 6.7 %fusion.61 = (f32[4,256]{1,0:T(4,128)S(1)}, f32[4,256]{1,0:T(4,128)S(1)}, f32[4,256]{1,0:T(4,128)S(1)}, f32[4,256]{1,0:T(4,128)S(1)}) fusion(f32[4,4,256]{2,1,0:T(4,128)S(1)} %get-tuple-element.370, f32[4,4,256]{2,1,0:T(4,128)S(1)} %bitcast.193, f32[4,256]{1,0:T(4,128)S(1)} %bitcast.198, f32[4,4,256]{2,1,0:T(4,128)S(1)} %get-tuple-element.375, ...), kind=kLoop, calls=%fused_computation.45.clone.1 | loop fusion | flops 35647488 | bytes 196608 | tf_op jit(solution)/shard_map/while/body/eval_jaxpr/reduce_sum | solution.py:71
  127.4 6.7 %fusion.61 = (f32[4,256]{1,0:T(4,128)S(1)}, f32[4,256]{1,0:T(4,128)S(1)}, f32[4,256]{1,0:T(4,128)S(1)}, f32[4,256]{1,0:T(4,128)S(1)}) fusion(f32[4,4,256]{2,1,0:T(4,128)S(1)} %get-tuple-element.370, f32[4,4,256]{2,1,0:T(4,128)S(1)} %bitcast.193, f32[4,256]{1,0:T(4,128)S(1)} %bitcast.198, f32[4,4,256]{2,1,0:T(4,128)S(1)} %get-tuple-element.375, ...), kind=kLoop, calls=%fused_computation.45.clone.1 | loop fusion | flops 35647488 | bytes 196608 | tf_op jit(solution)/shard_map/while/body/eval_jaxpr/reduce_sum | solution.py:71
  137.6 6.7 %fusion.61 = (f32[4,256]{1,0:T(4,128)S(1)}, f32[4,256]{1,0:T(4,128)S(1)}, f32[4,256]{1,0:T(4,128)S(1)}, f32[4,256]{1,0:T(4,128)S(1)}) fusion(f32[4,4,256]{2,1,0:T(4,128)S(1)} %get-tuple-element.370, f32[4,4,256]{2,1,0:T(4,128)S(1)} %bitcast.193, f32[4,256]{1,0:T(4,128)S(1)} %bitcast.198, f32[4,4,256]{2,1,0:T(4,128)S(1)} %get-tuple-element.375, ...), kind=kLoop, calls=%fused_computation.45.clone.1 | loop fusion | flops 35647488 | bytes 196608 | tf_op jit(solution)/shard_map/while/body/eval_jaxpr/reduce_sum | solution.py:71
  147.8 6.7 %fusion.61 = (f32[4,256]{1,0:T(4,128)S(1)}, f32[4,256]{1,0:T(4,128)S(1)}, f32[4,256]{1,0:T(4,128)S(1)}, f32[4,256]{1,0:T(4,128)S(1)}) fusion(f32[4,4,256]{2,1,0:T(4,128)S(1)} %get-tuple-element.370, f32[4,4,256]{2,1,0:T(4,128)S(1)} %bitcast.193, f32[4,256]{1,0:T(4,128)S(1)} %bitcast.198, f32[4,4,256]{2,1,0:T(4,128)S(1)} %get-tuple-element.375, ...), kind=kLoop, calls=%fused_computation.45.clone.1 | loop fusion | flops 35647488 | bytes 196608 | tf_op jit(solution)/shard_map/while/body/eval_jaxpr/reduce_sum | solution.py:71
  155.5 1.6 scatter_fusion
  157.2 2.1 %collective-permute-start.5 = (f32[7,2,256]{2,0,1:T(8,128)S(1)}, f32[7,2,256]{2,0,1:T(8,128)S(1)}, u32[]{:S(2)}, u32[]{:S(2)}) collective-permute-start(f32[7,2,256]{2,0,1:T(8,128)S(1)} %get-tuple-element.211), channel_id=1, source_target_pairs={{0,2},{1,3},{2,0},{3,1},{4,6},{5,7},{6,4},{7,5},{8,10},{9,11},{10,... | collective-permute-start | bytes 43016 | tf_op jit(solution)/shard_map/ppermute | solution.py:163
  159.4 1.7 %collective-permute-start.7 = (f32[7,2,256]{2,0,1:T(8,128)S(1)}, f32[7,2,256]{2,0,1:T(8,128)S(1)}, u32[]{:S(2)}, u32[]{:S(2)}) collective-permute-start(f32[7,2,256]{2,0,1:T(8,128)S(1)} %get-tuple-element.209), channel_id=1, source_target_pairs={{0,4},{1,5},{2,6},{3,7},{4,0},{5,1},{6,2},{7,3},{8,12},{9,13},{10,... | collective-permute-start | bytes 43016 | tf_op jit(solution)/shard_map/ppermute | solution.py:163
  161.1 2.6 %collective-permute-start.9 = (f32[7,2,256]{2,0,1:T(8,128)S(1)}, f32[7,2,256]{2,0,1:T(8,128)S(1)}, u32[]{:S(2)}, u32[]{:S(2)}) collective-permute-start(f32[7,2,256]{2,0,1:T(8,128)S(1)} %get-tuple-element.207), channel_id=1, source_target_pairs={{0,6},{1,7},{2,4},{3,5},{4,2},{5,3},{6,0},{7,1},{8,14},{9,15},{10,... | collective-permute-start | bytes 43016 | tf_op jit(solution)/shard_map/ppermute | solution.py:163
  164.3 1.5 collective-permute-done.9
  165.8 2.0 %collective-permute-done.10 = f32[7,2,256]{2,0,1:T(8,128)S(1)} collective-permute-done((f32[7,2,256]{2,0,1:T(8,128)S(1)}, f32[7,2,256]{2,0,1:T(8,128)S(1)}, u32[]{:S(2)}, u32[]{:S(2)}) %collective-permute-start.10) | collective-permute-done | bytes 14368 | tf_op jit(solution)/shard_map/ppermute | solution.py:163
  167.8 1.0 scatter_fusion.1
  168.9 1.5 scatter_fusion.2
  170.4 0.7 copy.55
  171.2 0.6 copy.108
  (387 shorter events, 46.4 us)
Async XLA Ops:
  0.6 15.0 %copy-start.2 = (s32[32]{0:T(128)S(1)}, s32[32]{0:T(128)}, u32[]{:S(2)}) copy-start(s32[32]{0:T(128)} %param.16) | copy-start | bytes 388
  0.6 15.1 %copy-start.3 = (s32[1,256]{1,0:T(1,128)S(1)}, s32[1,256]{1,0:T(1,128)}, u32[]{:S(2)}) copy-start(s32[1,256]{1,0:T(1,128)} %param.20) | copy-start | bytes 3076
  0.7 17.4 %copy-start.4 = (s32[32,3]{0,1:T(4,128)S(1)}, s32[32,3]{0,1:T(4,128)}, u32[]{:S(2)}) copy-start(s32[32,3]{0,1:T(4,128)} %param.18) | copy-start | bytes 1156
  0.7 17.5 %copy-start.1 = (f32[3,32,256]{2,1,0:T(8,128)S(1)}, f32[3,32,256]{2,1,0:T(8,128)}, u32[]{:S(2)}) copy-start(f32[3,32,256]{2,1,0:T(8,128)} %param.14) | copy-start | bytes 294916
  5.7 14.3 %all-to-all-start = ((f32[4,16,256]{2,0,1:T(4,128)}), f32[4,16,256]{2,0,1:T(4,128)S(1)}, u32[]{:S(2)}, u32[]{:S(2)}) async-start(f32[4,16,256]{2,0,1:T(4,128)} %multiply_bitcast_fusion.1), calls=%async_computation | async-start | bytes 131072 | tf_op jit(solution)/shard_map/all_to_all | solution.py:102
  10.9 7.5 %collective-permute-start = (f32[4,4,256]{2,0,1:T(4,128)S(1)}, f32[4,4,256]{2,0,1:T(4,128)S(1)}, u32[]{:S(2)}, u32[]{:S(2)}) collective-permute-start(f32[4,4,256]{2,0,1:T(4,128)S(1)} %get-tuple-element.204), channel_id=1, source_target_pairs={{0,8},{8,16},{16,24},{1,9},{9,17},{17,25},{2,10},{10,18},{18,26},{... | collective-permute-start | bytes 49160 | tf_op jit(solution)/shard_map/ppermute | solution.py:25
  14.4 5.6 %collective-permute-start.1 = (f32[4,4,256]{2,0,1:T(4,128)S(1)}, f32[4,4,256]{2,0,1:T(4,128)S(1)}, u32[]{:S(2)}, u32[]{:S(2)}) collective-permute-start(f32[4,4,256]{2,0,1:T(4,128)S(1)} %get-tuple-element.205), channel_id=1, source_target_pairs={{8,0},{16,8},{24,16},{9,1},{17,9},{25,17},{10,2},{18,10},{26,18},{... | collective-permute-start | bytes 49160 | tf_op jit(solution)/shard_map/ppermute | solution.py:27
  59.5 13.8 %all-to-all-start.1 = ((f32[9,16,256]{2,0,1:T(8,128)}), f32[9,16,256]{2,0,1:T(8,128)S(1)}, u32[]{:S(2)}, u32[]{:S(2)}) async-start(f32[9,16,256]{2,0,1:T(8,128)} %multiply_bitcast_fusion), calls=%async_computation.1 | async-start | bytes 524288 | tf_op jit(solution)/shard_map/all_to_all | solution.py:118
  63.7 5.5 %collective-permute-start.2 = (f32[9,4,256]{2,0,1:T(8,128)S(1)}, f32[9,4,256]{2,0,1:T(8,128)S(1)}, u32[]{:S(2)}, u32[]{:S(2)}) collective-permute-start(f32[9,4,256]{2,0,1:T(8,128)S(1)} %get-tuple-element.202), channel_id=1, source_target_pairs={{0,8},{8,16},{16,24},{1,9},{9,17},{17,25},{2,10},{10,18},{18,26},{... | collective-permute-start | bytes 110600 | tf_op jit(solution)/shard_map/ppermute | solution.py:25
  67.2 6.2 %collective-permute-start.3 = (f32[9,4,256]{2,0,1:T(8,128)S(1)}, f32[9,4,256]{2,0,1:T(8,128)S(1)}, u32[]{:S(2)}, u32[]{:S(2)}) collective-permute-start(f32[9,4,256]{2,0,1:T(8,128)S(1)} %get-tuple-element.203), channel_id=1, source_target_pairs={{8,0},{16,8},{24,16},{9,1},{17,9},{25,17},{10,2},{18,10},{26,18},{... | collective-permute-start | bytes 110600 | tf_op jit(solution)/shard_map/ppermute | solution.py:27
  73.4 81.8 %copy-start = (f32[3,32,256]{2,1,0:T(8,128)S(1)}, f32[3,32,256]{2,1,0:T(8,128)}, u32[]{:S(2)}) copy-start(f32[3,32,256]{2,1,0:T(8,128)} %param.13) | copy-start | bytes 294916
  73.5 81.8 %copy-start.5 = (f32[3]{0:T(128)S(1)}, f32[3]{0:T(128)}, u32[]{:S(2)}) copy-start(f32[3]{0:T(128)} %constant.123) | copy-start | bytes 40
  157.1 4.0 %collective-permute-start.4 = (f32[7,2,256]{2,0,1:T(8,128)S(1)}, f32[7,2,256]{2,0,1:T(8,128)S(1)}, u32[]{:S(2)}, u32[]{:S(2)}) collective-permute-start(f32[7,2,256]{2,0,1:T(8,128)S(1)} %get-tuple-element.212), channel_id=1, source_target_pairs={{0,1},{1,0},{2,3},{3,2},{4,5},{5,4},{6,7},{7,6},{8,9},{9,8},{10,11... | collective-permute-start | bytes 43016 | tf_op jit(solution)/shard_map/ppermute | solution.py:163
  157.2 6.5 %collective-permute-start.5 = (f32[7,2,256]{2,0,1:T(8,128)S(1)}, f32[7,2,256]{2,0,1:T(8,128)S(1)}, u32[]{:S(2)}, u32[]{:S(2)}) collective-permute-start(f32[7,2,256]{2,0,1:T(8,128)S(1)} %get-tuple-element.211), channel_id=1, source_target_pairs={{0,2},{1,3},{2,0},{3,1},{4,6},{5,7},{6,4},{7,5},{8,10},{9,11},{10,... | collective-permute-start | bytes 43016 | tf_op jit(solution)/shard_map/ppermute | solution.py:163
  159.3 4.5 %collective-permute-start.6 = (f32[7,2,256]{2,0,1:T(8,128)S(1)}, f32[7,2,256]{2,0,1:T(8,128)S(1)}, u32[]{:S(2)}, u32[]{:S(2)}) collective-permute-start(f32[7,2,256]{2,0,1:T(8,128)S(1)} %get-tuple-element.210), channel_id=1, source_target_pairs={{0,3},{1,2},{2,1},{3,0},{4,7},{5,6},{6,5},{7,4},{8,11},{9,10},{10,... | collective-permute-start | bytes 43016 | tf_op jit(solution)/shard_map/ppermute | solution.py:163
  159.4 4.5 %collective-permute-start.7 = (f32[7,2,256]{2,0,1:T(8,128)S(1)}, f32[7,2,256]{2,0,1:T(8,128)S(1)}, u32[]{:S(2)}, u32[]{:S(2)}) collective-permute-start(f32[7,2,256]{2,0,1:T(8,128)S(1)} %get-tuple-element.209), channel_id=1, source_target_pairs={{0,4},{1,5},{2,6},{3,7},{4,0},{5,1},{6,2},{7,3},{8,12},{9,13},{10,... | collective-permute-start | bytes 43016 | tf_op jit(solution)/shard_map/ppermute | solution.py:163
  161.1 3.2 %collective-permute-start.8 = (f32[7,2,256]{2,0,1:T(8,128)S(1)}, f32[7,2,256]{2,0,1:T(8,128)S(1)}, u32[]{:S(2)}, u32[]{:S(2)}) collective-permute-start(f32[7,2,256]{2,0,1:T(8,128)S(1)} %get-tuple-element.208), channel_id=1, source_target_pairs={{0,5},{1,4},{2,7},{3,6},{4,1},{5,0},{6,3},{7,2},{8,13},{9,12},{10,... | collective-permute-start | bytes 43016 | tf_op jit(solution)/shard_map/ppermute | solution.py:163
  161.1 4.6 %collective-permute-start.9 = (f32[7,2,256]{2,0,1:T(8,128)S(1)}, f32[7,2,256]{2,0,1:T(8,128)S(1)}, u32[]{:S(2)}, u32[]{:S(2)}) collective-permute-start(f32[7,2,256]{2,0,1:T(8,128)S(1)} %get-tuple-element.207), channel_id=1, source_target_pairs={{0,6},{1,7},{2,4},{3,5},{4,2},{5,3},{6,0},{7,1},{8,14},{9,15},{10,... | collective-permute-start | bytes 43016 | tf_op jit(solution)/shard_map/ppermute | solution.py:163
  163.7 4.1 %collective-permute-start.10 = (f32[7,2,256]{2,0,1:T(8,128)S(1)}, f32[7,2,256]{2,0,1:T(8,128)S(1)}, u32[]{:S(2)}, u32[]{:S(2)}) collective-permute-start(f32[7,2,256]{2,0,1:T(8,128)S(1)} %get-tuple-element.206), channel_id=1, source_target_pairs={{0,7},{1,6},{2,5},{3,4},{4,3},{5,2},{6,1},{7,0},{8,15},{9,14},{10,... | collective-permute-start | bytes 43016 | tf_op jit(solution)/shard_map/ppermute | solution.py:163
